TPU v7x, 256 devices: a whole 4x4x8 slice. The times are simulated.
256 devices in a mesh: frames: 8 (over y, x_lo), labels: 8 (over z), hidden: 4 (over x_hi, core).
Axes of the slice: x: 4 (x_hi: 2, x_lo: 2; x = x_hi * 2 + x_lo), y: 4, z: 8, core: 2. Of those that a mesh axis runs over, the one named last changes fastest.
Arguments:
- features: bfloat16 [1024, 1024], P('frames'), may hold values from -6 to 6
- up_weight: bfloat16 [1024, 4096], P(None, 'hidden'), may hold values from -0.1875 to 0.1875
- down_weight: bfloat16 [4096, 640], P('hidden'), may hold values from -0.09375 to 0.09375
- predictor: bfloat16 [512, 640], P(('labels', 'hidden')), may hold values from -4 to 4
- out_weight: bfloat16 [640, 1024], replicated, may hold values from -1.1 to 1.1
- blank_weight: float32 [1024, 512], P('frames', ('labels', 'hidden')), may hold values from 0 to 0.06
- label_weight: float32 [1024, 512], P('frames', ('labels', 'hidden')), may hold values from 0 to 0.06
- targets: int32 [512], P(('labels', 'hidden')), may hold values from 1 to 1023
Outputs:
- enc_grad: float32 [1024, 640], P(('frames', 'labels', 'hidden'))
- pred_grad: float32 [512, 640], P(('labels', 'hidden'))
- head_grad: float32 [1024, 640], P(('frames', 'labels', 'hidden'))
All inputs are finite; a program needn't handle non-finite values.
Results may differ from a plain program's by a relative error of at most 0.0023.
Values sent between devices are 32-bit elements; how exact they have to be, the bound alone decides.
A program may use at most 64 MiB of HBM per device.

v0:
```python
import math
import jax
import jax.numpy as jnp
from jax import lax
from jax.sharding import PartitionSpec as P


def on_device(
    features, up_weight, down_weight, predictor, out_weight, blank_weight, label_weight, targets
):
    frames_dev = features.shape[0]
    labels_dev = predictor.shape[0]
    joint_width = predictor.shape[1]
    vocab_size = out_weight.shape[1]
    hidden_act = jax.nn.relu(
        jnp.dot(features, up_weight, preferred_element_type=jnp.float32)
    ).astype(jnp.bfloat16)
    partial_enc = jnp.dot(hidden_act, down_weight, preferred_element_type=jnp.float32)
    encoded = lax.psum(partial_enc, "hidden")
    block_rows = min(frames_dev, max(1, 512 // labels_dev))
    while frames_dev % block_rows:
        block_rows = block_rows - 1
    pred_wide = predictor.astype(jnp.float32)
    vocab_ids = jnp.arange(vocab_size, dtype=jnp.int32)
    label_hot = (targets[:, None] == vocab_ids[None, :]).astype(jnp.float32)
    blank_hot = (vocab_ids == 0).astype(jnp.float32)
    cell_hot = jnp.broadcast_to(label_hot[None], (block_rows, labels_dev, vocab_size)).reshape(
        -1, vocab_size
    )

    def joint_step(pred_sum, inputs):
        enc_block, blank_block, label_block = inputs
        joint_cells = jnp.tanh(enc_block[:, None, :] + pred_wide[None, :, :]).astype(jnp.bfloat16)
        joint_cells = joint_cells.reshape(block_rows * labels_dev, joint_width)
        logits = jnp.dot(joint_cells, out_weight, preferred_element_type=jnp.float32)
        top_logit = jnp.max(logits, axis=1, keepdims=True)
        log_total = top_logit + jnp.log(jnp.sum(jnp.exp(logits - top_logit), axis=1, keepdims=True))
        probs = jnp.exp(logits - log_total)
        blank_flat = blank_block.reshape(-1, 1)
        label_flat = label_block.reshape(-1, 1)
        logit_grad = (
            (blank_flat + label_flat) * probs - blank_flat * blank_hot - label_flat * cell_hot
        ).astype(jnp.bfloat16)
        joint_grad = lax.dot_general(
            logit_grad, out_weight, (((1,), (1,)), ((), ())), preferred_element_type=jnp.float32
        )
        cells_wide = joint_cells.astype(jnp.float32)
        tanh_grad = (joint_grad * (1.0 - cells_wide * cells_wide)).reshape(
            block_rows, labels_dev, joint_width
        )
        return (
            pred_sum + jnp.sum(tanh_grad, axis=0),
            (joint_cells, logit_grad, jnp.sum(tanh_grad, axis=1)),
        )

    inputs = (
        encoded.reshape(-1, block_rows, joint_width),
        blank_weight.reshape(-1, block_rows, labels_dev),
        label_weight.reshape(-1, block_rows, labels_dev),
    )
    pred_sum, stacked = lax.scan(
        joint_step, jnp.zeros((labels_dev, joint_width), jnp.float32), inputs
    )
    joint_all = stacked[0].reshape(-1, joint_width)
    grad_all = stacked[1].reshape(-1, vocab_size)
    enc_parts = stacked[2].reshape(frames_dev, joint_width)
    enc_grad = lax.psum_scatter(enc_parts, ("labels", "hidden"), scatter_dimension=0, tiled=True)
    pred_grad = lax.psum(pred_sum, "frames")
    n_frames = lax.axis_size("frames")
    n_group = lax.axis_size("labels") * lax.axis_size("hidden")
    total_cells = frames_dev * n_frames * labels_dev * n_group
    head_sum = lax.psum_scatter(
        lax.dot_general(
            grad_all, joint_all, (((0,), (0,)), ((), ())), preferred_element_type=jnp.float32
        ),
        ("frames", "labels", "hidden"),
        scatter_dimension=0,
        tiled=True,
    )
    return (enc_grad, pred_grad, head_sum / math.sqrt(total_cells))


def solution(mesh):
    placed = (
        P("frames", None),
        P(None, "hidden"),
        P("hidden", None),
        P(("labels", "hidden"), None),
        P(),
        P("frames", ("labels", "hidden")),
        P("frames", ("labels", "hidden")),
        P(("labels", "hidden")),
    )
    return jax.shard_map(
        on_device,
        mesh=mesh,
        in_specs=placed,
        out_specs=(
            P(("frames", "labels", "hidden"), None),
            P(("labels", "hidden"), None),
            P(("frames", "labels", "hidden"), None),
        ),
        check_vma=False,
    )
```

profile of v0, /device:TPU:2, one launch (start us, length us, event | category | flops | bytes accessed | tf_op | source)
XLA Modules:
  0.0 650.8 jit_solution(10384635351723706598)
XLA Ops:
  7.3 1.5 copy-done
  8.8 2.8 fusion.8
  11.6 0.0 all-reduce.8.cloned.1.call-start
  11.7 0.1 copy.19
  11.8 0.1 copy.20
  12.0 0.1 fusion.10
  12.0 48.1 %all-reduce.6.cloned.1.call-done = f32[4,32,640]{2,1,0:T(8,128)} async-done(((f32[4,32,640]{2,1,0:T(8,128)}), f32[4,32,640]{2,1,0:T(8,128)}) %all-reduce.6.cloned.1.call-update) | async-done | bytes 327696 | tf_op jit(solution)/shard_map/psum | solution.py:19
  60.1 56.8 %while.17 = (s32[]{:T(128)}, f32[16,640]{1,0:T(8,128)S(1)}, bf16[4,512,640]{2,1,0:T(8,128)(2,1)}, bf16[4,512,1024]{2,1,0:T(8,128)(2,1)}, f32[4,32,640]{2,1,0:T(8...) while((s32[]{:T(128)}, f32[16,640]{1,0:T(8,128)S(1)}, ...), condition=%wide.region_6.7_spmd.clone, body=%wide.region_1.6_spmd.clone.sunk | while | flops 1350033408 | bytes 32403152 | solution.py:61
  60.1 0.9 dynamic-slice_bitcast_fusion.2
  61.0 0.3 tanh_convert_fusion.2
  61.3 2.4 fusion.33
  63.7 1.4 copy-done.1
  65.1 0.5 exponential_reduce_fusion.2
  65.6 0.1 reshape.133
  65.7 0.1 reshape.134
  65.8 3.4 bitcast_dynamic-update-slice_fusion.6
  69.2 2.2 bitcast_reduce_fusion.2
  71.4 0.6 bitcast_dynamic-update-slice_fusion.8
  72.0 1.4 reduce_sum.37
  73.4 0.9 bitcast_dynamic-update-slice_fusion.7
  74.3 0.9 dynamic-slice_bitcast_fusion.2
  75.2 0.3 tanh_convert_fusion.2
  75.5 2.4 fusion.33
  77.9 1.4 copy-done.1
  79.3 0.5 exponential_reduce_fusion.2
  79.8 0.1 reshape.133
  79.9 0.1 reshape.134
  80.0 3.4 bitcast_dynamic-update-slice_fusion.6
  83.4 2.1 bitcast_reduce_fusion.2
  85.6 0.6 bitcast_dynamic-update-slice_fusion.8
  86.2 1.4 reduce_sum.37
  87.6 0.9 bitcast_dynamic-update-slice_fusion.7
  88.6 0.9 dynamic-slice_bitcast_fusion.2
  89.4 0.3 tanh_convert_fusion.2
  89.7 2.4 fusion.33
  92.1 1.4 copy-done.1
  93.5 0.5 exponential_reduce_fusion.2
  94.0 0.1 reshape.133
  94.1 0.1 reshape.134
  94.2 3.4 bitcast_dynamic-update-slice_fusion.6
  97.6 2.2 bitcast_reduce_fusion.2
  99.8 0.6 bitcast_dynamic-update-slice_fusion.8
  100.4 1.4 reduce_sum.37
  101.8 0.9 bitcast_dynamic-update-slice_fusion.7
  102.8 0.9 dynamic-slice_bitcast_fusion.2
  103.6 0.3 tanh_convert_fusion.2
  103.9 2.4 fusion.33
  106.3 1.4 copy-done.1
  107.7 0.5 exponential_reduce_fusion.2
  108.2 0.1 reshape.133
  108.3 0.1 reshape.134
  108.4 3.4 bitcast_dynamic-update-slice_fusion.6
  111.8 2.2 bitcast_reduce_fusion.2
  114.0 0.6 bitcast_dynamic-update-slice_fusion.8
  114.6 1.4 reduce_sum.37
  116.0 0.9 bitcast_dynamic-update-slice_fusion.7
  117.0 8.0 %convolution_bitcast_fusion = f32[1024,640]{1,0:T(8,128)} fusion(bf16[4,512,1024]{2,1,0:T(8,128)(2,1)} %get-tuple-element.70, bf16[4,512,640]{2,1,0:T(8,128)(2,1)} %get-tuple-element.71), kind=kOutput, calls=%fused_computation.19 | convolution fusion | flops 2684354560 | bytes 9437184 | tf_op jit(solution)/shard_map/dot_general | solution.py:73
  125.1 0.6 copy-done.7
  125.7 0.6 dynamic-slice
  127.0 31.7 %psum.15 = f32[16,640]{1,0:T(8,128)} all-reduce(f32[16,640]{1,0:T(8,128)S(1)} %get-tuple-element.69), channel_id=1, replica_groups=mesh['frames'=8,'labels'=8,'hidden'=4] {'frames'}, use_global_device_ids=true, to_apply=%region_8.9 | all-reduce | flops 10240 | bytes 81920 | tf_op jit(solution)/shard_map/psum | solution.py:68
  158.7 214.1 %all-reduce.8.cloned.1.call-done = f32[128,640]{1,0:T(8,128)} async-done(((f32[128,640]{1,0:T(8,128)}), f32[128,640]{1,0:T(8,128)}) %all-reduce.8.cloned.1.call-update) | async-done | bytes 327696
  372.8 1.3 constant_dynamic-slice_fusion.2
  374.1 268.8 %all-reduce.10.cloned.1.call-done = f32[1024,640]{1,0:T(8,128)} async-done(((f32[1024,640]{1,0:T(8,128)}), f32[1024,640]{1,0:T(8,128)}) %all-reduce.10.cloned.1.call-update) | async-done | bytes 2621456
  642.9 1.3 dynamic-slice_multiply_fusion
  (52 shorter events, 0.4 us)
Async XLA Ops:
  7.2 1.6 copy-start
  7.2 4.5 copy-start.4
  7.2 4.6 copy-start.5
  7.2 4.7 copy-start.3
  7.2 4.7 copy-start.6
  7.2 52.9 %all-reduce.6.cloned.1.call-start = ((), (), s32[]{:S(2)}) async-start(), calls=%async_computation | async-start | bytes 655360 | tf_op jit(solution)/shard_map/psum | solution.py:19
  11.6 361.2 %all-reduce.8.cloned.1.call-start = ((), (), s32[]{:S(2)}) async-start(), calls=%async_computation.1 | async-start | bytes 655360
  63.7 1.4 copy-start.1
  65.8 3.4 copy-start.2
  77.9 1.4 copy-start.1
  80.0 3.5 copy-start.2
  92.1 1.4 copy-start.1
  94.2 3.4 copy-start.2
  106.3 1.4 copy-start.1
  108.4 3.4 copy-start.2
  117.0 526.0 %all-reduce.10.cloned.1.call-start = ((), (), s32[]{:S(2)}) async-start(), calls=%async_computation.2 | async-start | bytes 5242880
  125.1 0.7 copy-start.7
Sparse Core Ops, SparseCore 0:
  11.7 48.3 all-reduce.5
  117.1 255.6 all-reduce.7
  378.2 264.6 all-reduce.9
where the time goes:
time: 652 us; the launch traced here: 651 us
  waiting for transfers between devices  531 us (81%)
  blocking collectives  31.7 us (5%)
  matrix products  29 us (4%)
  other arithmetic  23.8 us (4%)
  local copies, waits for them, and re-layouts  20.3 us (3%)
  between operations  14.5 us (2%)
    unnamed x5, waiting for transfers between devices  483 us
    psum x1, waiting for transfers between devices, on_device(): encoded = lax.psum(partial_enc, 'hidden')  48.1 us
    psum x1, blocking collectives, on_device(): pred_grad = lax.psum(pred_sum, 'frames')  31.7 us
    dynamic_update_slice x4, other arithmetic, on_device(): lax.scan(joint_step, jnp.zeros((labels_dev, joint_width), jnp.float32), i...  13.6 us
  transfers between devices with their start and end apart: 3, of which 3 were waited for; matrix products, arithmetic and copies ran while one was open for 2% of the time, Pallas kernels for 0%

commit v1 on v0

--- a/solution.py
+++ b/solution.py
@@ -16,7 +16,7 @@
         jnp.dot(features, up_weight, preferred_element_type=jnp.float32)
     ).astype(jnp.bfloat16)
     partial_enc = jnp.dot(hidden_act, down_weight, preferred_element_type=jnp.float32)
-    encoded = lax.psum(partial_enc, "hidden")
+    encoded = jnp.sum(lax.all_gather(partial_enc, "hidden"), axis=0)
     block_rows = min(frames_dev, max(1, 512 // labels_dev))
     while frames_dev % block_rows:
         block_rows = block_rows - 1

time: 652 us -> 627 us (0.962)
  waiting for transfers between devices: 531 us -> 509 us
    psum x1 -> x0, waiting for transfers between devices: 48.1 us -> none  [on_device(): encoded = lax.psum(partial_enc, 'hidden')]
    all_gather x0 -> x1, waiting for transfers between devices: none -> 26.5 us  [on_device(): encoded = jnp.sum(lax.all_gather(partial_enc, 'hidden'), axis=0)]
where the time goes in v1:
time: 627 us
  waiting for transfers between devices  509 us (81%)
  blocking collectives  31.8 us (5%)
  matrix products  29 us (5%)
  other arithmetic  25.2 us (4%)
  local copies, waits for them, and re-layouts  16.8 us (3%)
  between operations  14.5 us (2%)
    unnamed x5, waiting for transfers between devices  483 us
    psum x1, blocking collectives, on_device(): pred_grad = lax.psum(pred_sum, 'frames')  31.8 us
    all_gather x1, waiting for transfers between devices, on_device(): encoded = jnp.sum(lax.all_gather(partial_enc, 'hidden'), axis=0)  26.5 us
    dynamic_update_slice x4, other arithmetic, on_device(): lax.scan(joint_step, jnp.zeros((labels_dev, joint_width), jnp.float32), i...  13.6 us
  transfers between devices with their start and end apart: 3, of which 3 were waited for; matrix products, arithmetic and copies ran while one was open for 2% of the time, Pallas kernels for 0%

profile of v1, /device:TPU:2, one launch (start us, length us, event | category | flops | bytes accessed | tf_op | source)
XLA Modules:
  0.0 626.7 jit_solution(15514025350204765328)
XLA Ops:
  7.2 0.0 all-gather.3.cloned.1.call-start
  7.3 1.5 copy-done
  8.8 2.9 fusion.8
  11.6 0.0 all-gather.3.cloned.1.call-update
  11.7 0.0 all-reduce.5.cloned.1.call-start
  11.8 0.1 copy.19
  11.9 0.1 copy.20
  12.0 0.1 fusion.10
  12.1 26.5 %all-gather.3.cloned.1.call-done = f32[512,640]{1,0:T(8,128)} async-done(((f32[128,640]{1,0:T(8,128)}), f32[512,640]{1,0:T(8,128)}) %all-gather.3.cloned.1.call-update) | async-done | bytes 1310736 | tf_op jit(solution)/shard_map/all_gather | solution.py:19
  38.6 1.4 reduce_sum.36
  40.0 53.2 %while.17 = (s32[]{:T(128)}, f32[16,640]{1,0:T(8,128)S(1)}, bf16[4,512,640]{2,1,0:T(8,128)(2,1)}, bf16[4,512,1024]{2,1,0:T(8,128)(2,1)}, f32[4,32,640]{2,1,0:T(8...) while((s32[]{:T(128)}, f32[16,640]{1,0:T(8,128)S(1)}, ...), condition=%wide.region_6.7_spmd.clone, body=%wide.region_1.6_spmd.clone.sunk | while | flops 1350033408 | bytes 32403152 | solution.py:61
  40.1 0.3 tanh_convert_fusion.2
  40.3 2.4 fusion.33
  42.7 1.4 copy-done.1
  44.1 0.5 exponential_reduce_fusion.2
  44.6 0.1 reshape.134
  44.7 0.1 reshape.135
  44.8 3.4 bitcast_dynamic-update-slice_fusion.6
  48.2 2.2 bitcast_reduce_fusion.2
  50.4 0.6 bitcast_dynamic-update-slice_fusion.8
  51.0 1.4 reduce_sum.47
  52.4 0.9 bitcast_dynamic-update-slice_fusion.7
  53.3 0.3 tanh_convert_fusion.2
  53.6 2.4 fusion.33
  56.0 1.4 copy-done.1
  57.4 0.5 exponential_reduce_fusion.2
  57.9 0.1 reshape.134
  58.0 0.1 reshape.135
  58.1 3.4 bitcast_dynamic-update-slice_fusion.6
  61.6 2.2 bitcast_reduce_fusion.2
  63.7 0.6 bitcast_dynamic-update-slice_fusion.8
  64.3 1.4 reduce_sum.47
  65.8 0.9 bitcast_dynamic-update-slice_fusion.7
  66.7 0.3 tanh_convert_fusion.2
  66.9 2.4 fusion.33
  69.3 1.4 copy-done.1
  70.7 0.5 exponential_reduce_fusion.2
  71.3 0.1 reshape.134
  71.3 0.1 reshape.135
  71.4 3.4 bitcast_dynamic-update-slice_fusion.6
  74.8 2.2 bitcast_reduce_fusion.2
  77.0 0.6 bitcast_dynamic-update-slice_fusion.8
  77.6 1.4 reduce_sum.47
  79.0 0.9 bitcast_dynamic-update-slice_fusion.7
  80.0 0.3 tanh_convert_fusion.2
  80.2 2.4 fusion.33
  82.6 1.4 copy-done.1
  84.0 0.5 exponential_reduce_fusion.2
  84.6 0.1 reshape.134
  84.6 0.1 reshape.135
  84.7 3.4 bitcast_dynamic-update-slice_fusion.6
  88.1 2.2 bitcast_reduce_fusion.2
  90.3 0.6 bitcast_dynamic-update-slice_fusion.8
  90.9 1.4 reduce_sum.47
  92.3 0.9 bitcast_dynamic-update-slice_fusion.7
  93.3 0.0 all-reduce.7.cloned.1.call-start
  93.3 8.0 %convolution_bitcast_fusion = f32[1024,640]{1,0:T(8,128)} fusion(bf16[4,512,1024]{2,1,0:T(8,128)(2,1)} %get-tuple-element.70, bf16[4,512,640]{2,1,0:T(8,128)(2,1)} %get-tuple-element.71), kind=kOutput, calls=%fused_computation.19 | convolution fusion | flops 2684354560 | bytes 9437184 | tf_op jit(solution)/shard_map/dot_general | solution.py:73
  101.4 0.6 copy-done.7
  102.1 0.6 dynamic-slice
  103.3 31.8 %psum.7 = f32[16,640]{1,0:T(8,128)} all-reduce(f32[16,640]{1,0:T(8,128)S(1)} %get-tuple-element.69), channel_id=1, replica_groups=mesh['frames'=8,'labels'=8,'hidden'=4] {'frames'}, use_global_device_ids=true, to_apply=%region_8.9 | all-reduce | flops 10240 | bytes 81920 | tf_op jit(solution)/shard_map/psum | solution.py:68
  135.0 213.7 %all-reduce.5.cloned.1.call-done = f32[128,640]{1,0:T(8,128)} async-done(((f32[128,640]{1,0:T(8,128)}), f32[128,640]{1,0:T(8,128)}) %all-reduce.5.cloned.1.call-update) | async-done | bytes 327696
  348.7 1.3 constant_dynamic-slice_fusion.2
  350.1 268.8 %all-reduce.7.cloned.1.call-done = f32[1024,640]{1,0:T(8,128)} async-done(((f32[1024,640]{1,0:T(8,128)}), f32[1024,640]{1,0:T(8,128)}) %all-reduce.7.cloned.1.call-update) | async-done | bytes 2621456
  618.9 1.3 dynamic-slice_multiply_fusion
  (53 shorter events, 0.3 us)
Async XLA Ops:
  7.2 1.6 copy-start
  7.2 4.6 copy-start.4
  7.2 4.7 copy-start.5
  7.2 4.8 copy-start.3
  7.2 4.8 copy-start.6
  7.2 31.4 %all-gather.3.cloned.1.call-start = ((), (), s32[]{:S(2)}) async-start(), calls=%async_computation | async-start | bytes 1638400 | tf_op jit(solution)/shard_map/all_gather | solution.py:19
  11.7 337.1 %all-reduce.5.cloned.1.call-start = ((), (), s32[]{:S(2)}) async-start(), calls=%async_computation.1 | async-start | bytes 655360
  42.7 1.4 copy-start.1
  44.8 3.4 copy-start.2
  56.0 1.4 copy-start.1
  58.1 3.5 copy-start.2
  69.3 1.4 copy-start.1
  71.4 3.4 copy-start.2
  82.6 1.4 copy-start.1
  84.7 3.4 copy-start.2
  93.3 525.6 %all-reduce.7.cloned.1.call-start = ((), (), s32[]{:S(2)}) async-start(), calls=%async_computation.2 | async-start | bytes 5242880
  101.4 0.7 copy-start.7
Sparse Core Ops, SparseCore 0:
  11.8 26.7 all-gather.2
  93.4 255.2 all-reduce.4
  354.2 264.6 all-reduce.6
